TPU v7x, 32 devices: a whole 2x2x4 slice. The times are simulated.
32 devices in a mesh: groups: 2 (over y), space: 4 (over x, core), tm: 4 (over z).
Axes of the slice: x: 2, y: 2, z: 4, core: 2. Of those that a mesh axis runs over, the one named last changes fastest.
Arguments:
- couplings: float32 [9, 4, 4, 2, 4, 96, 192], P(None, 'tm', 'space'), may hold values from -0.15625 to 0.15625
- source: float32 [4, 4, 2, 4, 96, 256], P('tm', 'space'), may hold values from -6 to 6
- initial: float32 [4, 4, 2, 4, 96, 256], P('tm', 'space'), may hold values from -6 to 6
- vectors: float32 [512, 4, 4, 2, 4, 192], P(None, 'tm', 'space'), may hold values from -0.0390625 to 0.0390625
- inverse_eigen: float32 [2, 512], replicated, may hold values from -20 to 20
Outputs:
- solution: float32 [8, 4, 2, 4, 96, 256], P(('groups', 'tm'), 'space'), parts along dimension 0
- residual: float32 [8, 4, 2, 4, 96, 256], P(('groups', 'tm'), 'space'), parts along dimension 0
There are 2 independent parts, one for each index of `groups`. A program takes and returns all parts, laid end to end along the dimension named above; an argument that names none is the same for every part. Nothing has to cross between parts.
All inputs are finite; a program needn't handle non-finite values.
Results may differ from a plain program's by a relative error of at most 0.0001.
Values sent between devices are 32-bit elements; how exact they have to be, the bound alone decides.
A program may use at most 64 MiB of HBM per device.

v0:
```python
import jax
import jax.numpy as jnp
from jax import lax
from jax.sharding import PartitionSpec as P

ITERS = 2


def with_halo(block, sides, width):
    for axis, dim in sides:
        count = lax.axis_size(axis)
        forward = [(i, i + 1) for i in range(count - 1)]
        forward.append((count - 1, 0))
        backward = [(target, source) for source, target in forward]
        low = lax.ppermute(
            lax.slice_in_dim(block, block.shape[dim] - width, None, axis=dim), axis, forward
        )
        high = lax.ppermute(lax.slice_in_dim(block, 0, width, axis=dim), axis, backward)
        block = jnp.concatenate([low, block, high], axis=dim)
    return block


def coupled(matrix, spinor):
    middle = spinor.shape[-1] // 2
    turned = jnp.concatenate([-spinor[..., middle:], spinor[..., :middle]], axis=-1)
    stacked = jnp.concatenate([spinor, turned], axis=-2)
    return jnp.einsum("tzyxij,tzyxjn->tzyxin", matrix, stacked, precision=lax.Precision.HIGHEST)


def layer_faces(spinor):
    time_padded = with_halo(spinor, (("tm", 0),), 1)
    space_padded = with_halo(spinor, (("space", 1),), 1)
    forward_t = time_padded[2:]
    backward_t = time_padded[:-2]
    forward_z = space_padded[:, 2:]
    backward_z = space_padded[:, :-2]
    return (forward_t, backward_t, forward_z, backward_z)


def apply_operator(spinor, couplings):
    forward_t, backward_t, forward_z, backward_z = layer_faces(spinor)
    at_last = lax.axis_index("tm") == lax.axis_size("tm") - 1
    at_first = lax.axis_index("tm") == 0
    sign_upper = jnp.where(at_last, -1.0, 1.0).astype(jnp.float32)
    sign_lower = jnp.where(at_first, -1.0, 1.0).astype(jnp.float32)
    forward_t = forward_t.at[-1].multiply(sign_upper)
    backward_t = backward_t.at[0].multiply(sign_lower)
    neighbours = [
        spinor,
        jnp.roll(spinor, -1, 3),
        jnp.roll(spinor, 1, 3),
        jnp.roll(spinor, -1, 2),
        jnp.roll(spinor, 1, 2),
        forward_z,
        backward_z,
        forward_t,
        backward_t,
    ]
    summed = jnp.zeros_like(spinor)
    for direction in range(9):
        summed = summed + coupled(couplings[direction], neighbours[direction])
    return summed


def scale_coeffs(coefficients, eigen_part):
    middle = coefficients.shape[-1] // 2
    eigen_real = eigen_part[0][:, None]
    eigen_imag = eigen_part[1][:, None]
    coef_real = coefficients[:, :middle]
    coef_imag = coefficients[:, middle:]
    scaled_real = eigen_real * coef_real - eigen_imag * coef_imag
    scaled_imag = eigen_real * coef_imag + eigen_imag * coef_real
    return jnp.concatenate([scaled_real, scaled_imag], axis=-1)


def deflate(residual, vectors, inverse_eigen):
    middle = residual.shape[-1] // 2
    number = vectors.shape[0]
    negated = jnp.concatenate([residual[..., middle:], -residual[..., :middle]], axis=-1)
    stacked = jnp.concatenate([residual, negated], axis=-2)
    partial_value = jnp.dot(
        vectors.reshape(number, -1),
        stacked.reshape(-1, stacked.shape[-1]),
        precision=lax.Precision.HIGHEST,
        preferred_element_type=jnp.float32,
    )
    over_time = lax.psum(partial_value, "tm")
    owned = lax.psum_scatter(over_time, "space", scatter_dimension=0, tiled=True)
    owned_rows = owned.shape[0]
    offset = lax.axis_index("space") * owned_rows
    eigen_part = lax.dynamic_slice_in_dim(inverse_eigen, offset, owned_rows, 1)
    scaled = lax.all_gather(scale_coeffs(owned, eigen_part), "space", axis=0, tiled=True)
    dstack = jnp.stack(
        [scaled, jnp.concatenate([-scaled[:, middle:], scaled[:, :middle]], axis=-1)]
    )
    halves = vectors.reshape(vectors.shape[:-1] + (2, vectors.shape[-1] // 2))
    return jnp.einsum("ktzyxci,ckn->tzyxin", halves, dstack, precision=lax.Precision.HIGHEST)


def shards(couplings, source, initial, vectors, inverse_eigen):
    iterate = initial
    residual = source
    for sweep in range(ITERS):
        residual = source - apply_operator(iterate, couplings)
        iterate = iterate + deflate(residual, vectors, inverse_eigen) + 0.5 * residual
    return (iterate, residual)


def solution(mesh):
    in_specs = (
        P(None, "tm", "space", None, None, None, None),
        P("tm", "space", None, None, None, None),
        P("tm", "space", None, None, None, None),
        P(None, "tm", "space", None, None, None),
        P(),
    )
    out_specs = (
        P(("groups", "tm"), "space", None, None, None, None),
        P(("groups", "tm"), "space", None, None, None, None),
    )
    return jax.shard_map(shards, mesh=mesh, in_specs=in_specs, out_specs=out_specs, check_vma=False)
```

profile of v0, /device:TPU:1, one launch (start us, length us, event | category | flops | bytes accessed | tf_op | source)
XLA Modules:
  0.0 262.8 jit_solution(13960371233287765386)
XLA Ops:
  7.2 4.2 %collective-permute-start.2 = (f32[1,1,2,4,96,256]{5,4,3,2,1,0:T(8,128)}, f32[1,1,2,4,96,256]{5,4,3,2,1,0:T(8,128)}, u32[]{:S(2)}, u32[]{:S(2)}) collective-permute-start(f32[1,1,2,4,96,256]{5,4,3,2,1,0:T(8,128)} %param.15), channel_id=1, source_target_pairs={{1,0},{2,1},{3,2},{0,3},{5,4},{6,5},{7,6},{4,7},{9,8},{10,9},{11,1... | collective-permute-start | bytes 2359304 | tf_op jit(solution)/shard_map/ppermute | solution.py:18
  11.4 2.1 collective-permute-start.1
  13.5 1.2 fusion.237
  14.7 3.0 %fusion.152 = f32[2,4,256,96]{2,3,1,0:T(8,128)} fusion(f32[1,1,1,4,96,256]{5,4,3,2,1,0:T(8,128)S(1)} %get-tuple-element.79, f32[1,1,1,4,96,256]{5,4,3,2,1,0:T(8,128)S(1)} %get-tuple-element.78, f32[1,1,2,4,96,128]{5,4,3,2,1,0:T(8,128)S(1)} %fusion.203, f32[9,1,1,2,4,96,192]{6,5,4,3,2,1,0:T(8,128)} %param.13), kind=kOutput, calls=%fused_computation.154 | convolution fusion | flops 454557696 | bytes 2752512 | tf_op jit(solution)/shard_map/tzyxij,tzyxjn->tzyxin/dot_general | solution.py:27
  17.7 3.1 %fusion.154 = f32[2,4,256,96]{2,3,1,0:T(8,128)} fusion(f32[1,1,1,4,96,256]{5,4,3,2,1,0:T(8,128)S(1)} %get-tuple-element.79, f32[1,1,1,4,96,256]{5,4,3,2,1,0:T(8,128)S(1)} %get-tuple-element.78, f32[1,1,2,4,96,128]{5,4,3,2,1,0:T(8,128)S(1)} %fusion.203, f32[9,1,1,2,4,96,192]{6,5,4,3,2,1,0:T(8,128)} %param.13), kind=kOutput, calls=%fused_computation.155 | convolution fusion | flops 454557696 | bytes 2752512 | tf_op jit(solution)/shard_map/tzyxij,tzyxjn->tzyxin/dot_general | solution.py:27
  21.8 3.0 %fusion.31 = f32[2,4,256,96]{2,3,1,0:T(8,128)} fusion(f32[1,1,2,1,96,256]{5,4,3,2,1,0:T(8,128)S(1)} %get-tuple-element.73, f32[1,1,2,3,96,256]{5,4,3,2,1,0:T(8,128)S(1)} %get-tuple-element.75, f32[1,1,2,4,96,128]{5,4,3,2,1,0:T(8,128)S(1)} %fusion.207, f32[9,1,1,2,4,96,192]{6,5,4,3,2,1,0:T(8,128)} %param.13), kind=kOutput, calls=%fused_computation.34 | convolution fusion | flops 454557696 | bytes 2752512 | tf_op jit(solution)/shard_map/tzyxij,tzyxjn->tzyxin/dot_general | solution.py:27
  27.0 2.9 %fusion.111 = f32[2,4,256,96]{2,3,1,0:T(8,128)S(1)} fusion(f32[2,4,256,96]{2,3,1,0:T(8,128)} %fusion.31, f32[1,1,2,4,96,128]{5,4,3,2,1,0:T(8,128)} %get-tuple-element.77, f32[1,1,2,4,96,128]{5,4,3,2,1,0:T(8,128)} %get-tuple-element.76, f32[1,1,2,4,96,256]{5,4,3,2,1,0:T(8,128)S(1)} %copy-done.2, f32[9,1,1,2,4,96,192]{6,5,4,3,2,1,0:T(8,128)} %param.13), kind=kOutput, calls=%fused_computation.125 | convolution fusion | flops 453967872 | bytes 3932160 | tf_op jit(solution)/shard_map/tzyxij,tzyxjn->tzyxin/dot_general | solution.py:27
  29.9 2.2 fusion.127
  32.2 1.2 broadcast_multiply_fusion.3
  33.4 12.3 %collective-permute-done.3 = f32[1,1,2,4,96,256]{5,4,3,2,1,0:T(8,128)} collective-permute-done((f32[1,1,2,4,96,256]{5,4,3,2,1,0:T(8,128)}, f32[1,1,2,4,96,256]{5,4,3,2,1,0:T(8,128)}, u32[]{:S(2)}, u32[]{:S(2)}) %collective-permute-start.3) | collective-permute-done | bytes 786464 | tf_op jit(solution)/shard_map/ppermute | solution.py:15
  45.7 1.2 broadcast_multiply_fusion.1
  47.0 1.2 slice_negate_fusion.9
  48.2 2.2 fusion.57
  50.4 2.2 fusion.62
  52.7 1.2 slice_negate_fusion.10
  53.8 2.5 fusion.52
  56.4 2.7 %fusion.139 = f32[1,1,2,4,96,256]{5,4,3,2,1,0:T(8,128)S(1)} fusion(f32[1,1,2,4,96,256]{5,4,3,2,1,0:T(8,128)S(1)} %copy-done.10, f32[2,4,256,96]{2,3,1,0:T(8,128)S(1)} %fusion.62, f32[2,4,256,96]{2,3,1,0:T(8,128)S(1)} %fusion.57, f32[2,4,256,96]{2,3,1,0:T(8,128)S(1)} %fusion.52, f32[2,4,256,96]{2,3,1,0:T(8,128)S(1)} %fusion.127, ...), kind=kOutput, calls=%fused_computation.143 | convolution fusion | flops 454754304 | bytes 7077888 | tf_op jit(solution)/shard_map/tzyxij,tzyxjn->tzyxin/dot_general | solution.py:27
  59.9 4.0 %fusion.142 = f32[512,256]{0,1:T(8,128)} fusion(f32[512,1,1,2,4,192]{0,5,4,3,2,1:T(8,128)S(1)} %copy-done, f32[1,1,2,4,96,128]{5,4,3,2,1,0:T(8,128)S(1)} %get-tuple-element.69, f32[1,1,2,4,96,128]{5,4,3,2,1,0:T(8,128)S(1)} %get-tuple-element.68, f32[1,1,2,4,96,256]{5,4,3,2,1,0:T(8,128)S(1)} %fusion.139), kind=kOutput, calls=%fused_computation.146 | convolution fusion | flops 2416705536 | bytes 5242880 | tf_op jit(solution)/shard_map/dot_general | solution.py:81
  64.7 21.2 %reduce-scatter.3.cloned.1.call-done = f32[128,256]{0,1:T(8,128)} async-done(((f32[512,256]{0,1:T(8,128)}), f32[128,256]{0,1:T(8,128)}) %reduce-scatter.3.cloned.1.call-update) | async-done | bytes 131088 | tf_op jit(solution)/shard_map/reduce_scatter | solution.py:88
  85.9 34.9 %all-reduce.3.cloned.1.call-done = f32[128,256]{0,1:T(8,128)} async-done(((f32[128,256]{0,1:T(8,128)}), f32[128,256]{0,1:T(8,128)}) %all-reduce.3.cloned.1.call-update) | async-done | bytes 131088 | tf_op jit(solution)/shard_map/psum | solution.py:87
  121.8 9.9 %all_gather.6 = f32[512,256]{0,1:T(8,128)S(1)} all-gather(f32[128,256]{0,1:T(8,128)S(1)} %pad_maximum_fusion.6), channel_id=1, replica_groups=mesh['groups'=2,'space'=4,'tm'=4] {'space'}, dimensions={0}, use_global_device_ids=true | all-gather | bytes 655360 | tf_op jit(solution)/shard_map/all_gather | solution.py:92
  131.8 3.6 %multiply_add_fusion.1 = (f32[1,1,2,4,96,256]{5,4,3,2,1,0:T(8,128)S(1)}, f32[1,1,2,4,96,256]{5,4,3,2,1,0:T(8,128)}) fusion(f32[1,1,2,4,96,256]{5,4,3,2,1,0:T(8,128)S(1)} %copy-done.5, f32[1,1,2,4,96,256]{5,4,3,2,1,0:T(8,128)S(1)} %copy-done.3, f32[512,2,4,2,96]{0,4,3,2,1:T(8,128)S(1)} %bitcast.221, f32[1,512,256]{1,2,0:T(8,128)S(1)} %maximum_bitcast_fusion.62, ...), kind=kOutput, calls=%fused_computation.189 | convolution fusion | flops 2416771072 | bytes 7340032 | tf_op jit(solution)/shard_map/ktzyxci,ckn->tzyxin/dot_general | solution.py:97
  138.4 1.8 collective-permute-start.6
  143.8 13.8 %collective-permute-done.6 = f32[1,1,2,4,96,256]{5,4,3,2,1,0:T(8,128)S(1)} collective-permute-done((f32[1,1,2,4,96,256]{5,4,3,2,1,0:T(8,128)S(1)}, f32[1,1,2,4,96,256]{5,4,3,2,1,0:T(8,128)S(1)}, u32[]{:S(2)}, u32[]{:S(2)}) %collective-permute-start.6) | collective-permute-done | bytes 786464 | tf_op jit(solution)/shard_map/ppermute | solution.py:18
  157.7 18.3 %collective-permute-done.7 = f32[1,1,2,4,96,256]{5,4,3,2,1,0:T(8,128)S(1)} collective-permute-done((f32[1,1,2,4,96,256]{5,4,3,2,1,0:T(8,128)S(1)}, f32[1,1,2,4,96,256]{5,4,3,2,1,0:T(8,128)S(1)}, u32[]{:S(2)}, u32[]{:S(2)}) %collective-permute-start.7) | collective-permute-done | bytes 786464 | tf_op jit(solution)/shard_map/ppermute | solution.py:15
  178.6 1.1 fusion.89
  179.7 1.3 fusion.138
  181.9 3.8 %fusion.145 = f32[512,256]{0,1:T(8,128)} fusion(f32[512,1,1,2,4,192]{0,5,4,3,2,1:T(8,128)S(1)} %copy-done, f32[1,1,2,4,96,128]{5,4,3,2,1,0:T(8,128)S(1)} %get-tuple-element.51, f32[1,1,2,4,96,128]{5,4,3,2,1,0:T(8,128)S(1)} %get-tuple-element.50, f32[1,1,2,4,96,256]{5,4,3,2,1,0:T(8,128)S(1)} %fusion.138), kind=kOutput, calls=%fused_computation.147 | convolution fusion | flops 2416705536 | bytes 5242880 | tf_op jit(solution)/shard_map/dot_general | solution.py:81
  185.8 20.8 %reduce-scatter.5.cloned.1.call-done = f32[128,256]{0,1:T(8,128)} async-done(((f32[512,256]{0,1:T(8,128)}), f32[128,256]{0,1:T(8,128)}) %reduce-scatter.5.cloned.1.call-update) | async-done | bytes 131088 | tf_op jit(solution)/shard_map/reduce_scatter | solution.py:88
  206.5 34.8 %all-reduce.5.cloned.1.call-done = f32[128,256]{0,1:T(8,128)} async-done(((f32[128,256]{0,1:T(8,128)}), f32[128,256]{0,1:T(8,128)}) %all-reduce.5.cloned.1.call-update) | async-done | bytes 131088 | tf_op jit(solution)/shard_map/psum | solution.py:87
  242.3 10.2 %all_gather.7 = f32[512,256]{0,1:T(8,128)S(1)} all-gather(f32[128,256]{0,1:T(8,128)S(1)} %pad_maximum_fusion.7), channel_id=1, replica_groups=mesh['groups'=2,'space'=4,'tm'=4] {'space'}, dimensions={0}, use_global_device_ids=true | all-gather | bytes 655360 | tf_op jit(solution)/shard_map/all_gather | solution.py:92
  252.6 3.6 %multiply_add_fusion = f32[1,1,2,4,96,256]{5,4,3,2,1,0:T(8,128)} fusion(f32[1,1,2,4,96,256]{5,4,3,2,1,0:T(8,128)S(1)} %copy-done.8, f32[512,2,4,2,96]{0,4,3,2,1:T(8,128)S(1)} %bitcast.222, f32[1,512,256]{1,2,0:T(8,128)S(1)} %maximum_bitcast_fusion.63, f32[1,512,256]{1,2,0:T(8,128)S(1)} %bitcast.225, f32[1,1,2,4,96,256]{5,4,3,2,1,0:T(8,128)S(1)} %copy-done.12, ...), kind=kOutput, calls=%fused_computation.188 | convolution fusion | flops 2417164288 | bytes 7340032 | tf_op jit(solution)/shard_map/ktzyxci,ckn->tzyxin/dot_general | solution.py:97
  (93 shorter events, 17.1 us)
Async XLA Ops:
  7.2 52.8 %copy-start = (f32[512,1,1,2,4,192]{0,5,4,3,2,1:T(8,128)S(1)}, f32[512,1,1,2,4,192]{0,5,4,3,2,1:T(8,128)}, u32[]{:S(2)}) copy-start(f32[512,1,1,2,4,192]{0,5,4,3,2,1:T(8,128)} %param.16) | copy-start | bytes 9437188
  7.2 78.6 %reduce-scatter.3.cloned.1.call-start = ((), (), s32[]{:S(2)}) async-start(), calls=%async_computation.2 | async-start | bytes 655360 | tf_op jit(solution)/shard_map/reduce_scatter | solution.py:88
  7.2 24.9 %collective-permute-start.2 = (f32[1,1,2,4,96,256]{5,4,3,2,1,0:T(8,128)}, f32[1,1,2,4,96,256]{5,4,3,2,1,0:T(8,128)}, u32[]{:S(2)}, u32[]{:S(2)}) collective-permute-start(f32[1,1,2,4,96,256]{5,4,3,2,1,0:T(8,128)} %param.15), channel_id=1, source_target_pairs={{1,0},{2,1},{3,2},{0,3},{5,4},{6,5},{7,6},{4,7},{9,8},{10,9},{11,1... | collective-permute-start | bytes 2359304 | tf_op jit(solution)/shard_map/ppermute | solution.py:18
  11.4 34.3 %collective-permute-start.3 = (f32[1,1,2,4,96,256]{5,4,3,2,1,0:T(8,128)}, f32[1,1,2,4,96,256]{5,4,3,2,1,0:T(8,128)}, u32[]{:S(2)}, u32[]{:S(2)}) collective-permute-start(f32[1,1,2,4,96,256]{5,4,3,2,1,0:T(8,128)} %param.15), channel_id=1, source_target_pairs={{0,1},{1,2},{2,3},{3,0},{4,5},{5,6},{6,7},{7,4},{8,9},{9,10},{10,1... | collective-permute-start | bytes 2359304 | tf_op jit(solution)/shard_map/ppermute | solution.py:15
  11.4 35.6 %collective-permute-start.1 = (f32[1,1,2,4,96,256]{5,4,3,2,1,0:T(8,128)}, f32[1,1,2,4,96,256]{5,4,3,2,1,0:T(8,128)}, u32[]{:S(2)}, u32[]{:S(2)}) collective-permute-start(f32[1,1,2,4,96,256]{5,4,3,2,1,0:T(8,128)} %param.15), channel_id=1, source_target_pairs={{0,4},{4,8},{8,12},{12,0},{1,5},{5,9},{9,13},{13,1},{2,6},{6,10},{... | collective-permute-start | bytes 2359304 | tf_op jit(solution)/shard_map/ppermute | solution.py:15
  13.5 39.2 %collective-permute-start = (f32[1,1,2,4,96,256]{5,4,3,2,1,0:T(8,128)}, f32[1,1,2,4,96,256]{5,4,3,2,1,0:T(8,128)}, u32[]{:S(2)}, u32[]{:S(2)}) collective-permute-start(f32[1,1,2,4,96,256]{5,4,3,2,1,0:T(8,128)} %param.15), channel_id=1, source_target_pairs={{4,0},{8,4},{12,8},{0,12},{5,1},{9,5},{13,9},{1,13},{6,2},{10,6},{... | collective-permute-start | bytes 2359304 | tf_op jit(solution)/shard_map/ppermute | solution.py:18
  17.7 3.1 %copy-start.1 = (f32[1,1,2,4,96,256]{5,4,3,2,1,0:T(8,128)S(1)}, f32[1,1,2,4,96,256]{5,4,3,2,1,0:T(8,128)}, u32[]{:S(2)}) copy-start(f32[1,1,2,4,96,256]{5,4,3,2,1,0:T(8,128)} %param.15) | copy-start | bytes 2359300
  25.8 1.2 copy-start.2
  27.0 2.9 %copy-start.9 = (f32[1,1,2,3,96,256]{5,4,3,2,1,0:T(8,128)S(1)}, f32[1,1,2,3,96,256]{5,4,3,2,1,0:T(8,128)}, u32[]{:S(2)}) copy-start(f32[1,1,2,3,96,256]{5,4,3,2,1,0:T(8,128)} %get-tuple-element.74) | copy-start | bytes 1769476
  27.0 2.9 %copy-start.13 = (f32[2,4,256,96]{2,3,1,0:T(8,128)S(1)}, f32[2,4,256,96]{2,3,1,0:T(8,128)}, u32[]{:S(2)}) copy-start(f32[2,4,256,96]{2,3,1,0:T(8,128)} %fusion.152) | copy-start | bytes 2359300
  27.0 2.9 %copy-start.14 = (f32[2,4,256,96]{2,3,1,0:T(8,128)S(1)}, f32[2,4,256,96]{2,3,1,0:T(8,128)}, u32[]{:S(2)}) copy-start(f32[2,4,256,96]{2,3,1,0:T(8,128)} %fusion.154) | copy-start | bytes 2359300
  53.8 2.5 copy-start.10
  59.0 0.9 copy-start.4
  63.9 56.9 %all-reduce.3.cloned.1.call-start = ((), (), s32[]{:S(2)}) async-start(), calls=%async_computation.3 | async-start | bytes 262144 | tf_op jit(solution)/shard_map/psum | solution.py:87
  85.8 120.7 %reduce-scatter.5.cloned.1.call-start = ((), (), s32[]{:S(2)}) async-start(), calls=%async_computation.4 | async-start | bytes 655360 | tf_op jit(solution)/shard_map/reduce_scatter | solution.py:88
  121.7 10.0 %copy-start.3 = (f32[1,1,2,4,96,256]{5,4,3,2,1,0:T(8,128)S(1)}, f32[1,1,2,4,96,256]{5,4,3,2,1,0:T(8,128)}, u32[]{:S(2)}) copy-start(f32[1,1,2,4,96,256]{5,4,3,2,1,0:T(8,128)} %param.15) | copy-start | bytes 2359300
  121.8 10.0 %copy-start.5 = (f32[1,1,2,4,96,256]{5,4,3,2,1,0:T(8,128)S(1)}, f32[1,1,2,4,96,256]{5,4,3,2,1,0:T(8,128)}, u32[]{:S(2)}) copy-start(f32[1,1,2,4,96,256]{5,4,3,2,1,0:T(8,128)} %copy-done.4) | copy-start | bytes 2359300
  131.7 4.0 %slice-start = ((s8[7077888]{0:T(1024)(128)(4,1)}), s8[4194304]{0:T(1024)(128)(4,1)S(1)}, s32[]{:S(2)}) async-start(s8[7077888]{0:T(1024)(128)(4,1)} %bitcast.223), calls=%async_computation.6 | async-start | bytes 8388608
  131.8 3.9 %slice-start.1 = ((s8[7077888]{0:T(1024)(128)(4,1)}), s8[2883584]{0:T(1024)(128)(4,1)S(1)}, s32[]{:S(2)}) async-start(s8[7077888]{0:T(1024)(128)(4,1)} %bitcast.223), calls=%async_computation.7 | async-start | bytes 5767168
  137.8 38.4 %collective-permute-start.5 = (f32[1,1,2,4,96,256]{5,4,3,2,1,0:T(8,128)S(1)}, f32[1,1,2,4,96,256]{5,4,3,2,1,0:T(8,128)S(1)}, u32[]{:S(2)}, u32[]{:S(2)}) collective-permute-start(f32[1,1,2,4,96,256]{5,4,3,2,1,0:T(8,128)S(1)} %get-tuple-element.96), channel_id=1, source_target_pairs={{0,4},{4,8},{8,12},{12,0},{1,5},{5,9},{9,13},{13,1},{2,6},{6,10},{... | collective-permute-start | bytes 2359304 | tf_op jit(solution)/shard_map/ppermute | solution.py:15
  138.4 19.2 %collective-permute-start.6 = (f32[1,1,2,4,96,256]{5,4,3,2,1,0:T(8,128)S(1)}, f32[1,1,2,4,96,256]{5,4,3,2,1,0:T(8,128)S(1)}, u32[]{:S(2)}, u32[]{:S(2)}) collective-permute-start(f32[1,1,2,4,96,256]{5,4,3,2,1,0:T(8,128)S(1)} %get-tuple-element.96), channel_id=1, source_target_pairs={{1,0},{2,1},{3,2},{0,3},{5,4},{6,5},{7,6},{4,7},{9,8},{10,9},{11,1... | collective-permute-start | bytes 2359304 | tf_op jit(solution)/shard_map/ppermute | solution.py:18
  140.3 35.7 %collective-permute-start.7 = (f32[1,1,2,4,96,256]{5,4,3,2,1,0:T(8,128)S(1)}, f32[1,1,2,4,96,256]{5,4,3,2,1,0:T(8,128)S(1)}, u32[]{:S(2)}, u32[]{:S(2)}) collective-permute-start(f32[1,1,2,4,96,256]{5,4,3,2,1,0:T(8,128)S(1)} %get-tuple-element.96), channel_id=1, source_target_pairs={{0,1},{1,2},{2,3},{3,0},{4,5},{5,6},{6,7},{7,4},{8,9},{9,10},{10,1... | collective-permute-start | bytes 2359304 | tf_op jit(solution)/shard_map/ppermute | solution.py:15
  140.3 38.2 %collective-permute-start.4 = (f32[1,1,2,4,96,256]{5,4,3,2,1,0:T(8,128)S(1)}, f32[1,1,2,4,96,256]{5,4,3,2,1,0:T(8,128)S(1)}, u32[]{:S(2)}, u32[]{:S(2)}) collective-permute-start(f32[1,1,2,4,96,256]{5,4,3,2,1,0:T(8,128)S(1)} %get-tuple-element.96), channel_id=1, source_target_pairs={{4,0},{8,4},{12,8},{0,12},{5,1},{9,5},{13,9},{1,13},{6,2},{10,6},{... | collective-permute-start | bytes 2359304 | tf_op jit(solution)/shard_map/ppermute | solution.py:18
  178.6 1.1 copy-start.11
  181.0 0.9 copy-start.7
  185.7 55.7 %all-reduce.5.cloned.1.call-start = ((), (), s32[]{:S(2)}) async-start(), calls=%async_computation.5 | async-start | bytes 262144 | tf_op jit(solution)/shard_map/psum | solution.py:87
  242.3 10.3 %copy-start.6 = (f32[1,1,2,4,96,256]{5,4,3,2,1,0:T(8,128)S(1)}, f32[1,1,2,4,96,256]{5,4,3,2,1,0:T(8,128)}, u32[]{:S(2)}) copy-start(f32[1,1,2,4,96,256]{5,4,3,2,1,0:T(8,128)} %copy-done.4) | copy-start | bytes 2359300
  242.3 10.3 %copy-start.8 = (f32[1,1,2,4,96,256]{5,4,3,2,1,0:T(8,128)S(1)}, f32[1,1,2,4,96,256]{5,4,3,2,1,0:T(8,128)}, u32[]{:S(2)}) copy-start(f32[1,1,2,4,96,256]{5,4,3,2,1,0:T(8,128)} %copy-done.7) | copy-start | bytes 2359300
  242.3 10.3 %copy-start.12 = (f32[1,1,2,4,96,256]{5,4,3,2,1,0:T(8,128)S(1)}, f32[1,1,2,4,96,256]{5,4,3,2,1,0:T(8,128)}, u32[]{:S(2)}) copy-start(f32[1,1,2,4,96,256]{5,4,3,2,1,0:T(8,128)} %get-tuple-element.97) | copy-start | bytes 2359300
Sparse Core Ops, SparseCore 0:
  64.0 21.7 reduce-scatter.2
  88.1 32.6 all-reduce.2
  185.8 20.6 reduce-scatter.4
  208.7 32.6 all-reduce.4
where the time goes:
time: 264 us; the launch traced here: 263 us
  waiting for transfers between devices  156 us (59%)
  matrix products  48.7 us (18%)
  blocking collectives  20.1 us (8%)
  between operations  14.4 us (5%)
  other arithmetic  9.61 us (4%)
  starting transfers between devices  9.09 us (3%)
  local copies, waits for them, and re-layouts  4.8 us (2%)
    psum x2, waiting for transfers between devices, deflate(): over_time = lax.psum(partial_value, 'tm')  69.8 us
    reduce_scatter x2, waiting for transfers between devices, deflate(): lax.psum_scatter(over_time, 'space', scatter_dimension=0, tiled=True)  41.9 us
    dot_general x18, matrix products, coupled(): jnp.einsum('tzyxij,tzyxjn->tzyxin', matrix, stacked, precision=lax.Precis...  33.7 us
    ppermute x4, waiting for transfers between devices, with_halo(): lax.ppermute(lax.slice_in_dim(block, block.shape[dim] - width, None, axis...  30.5 us
    all_gather x2, blocking collectives, deflate(): lax.all_gather(scale_coeffs(owned, eigen_part), 'space', axis=0, tiled=True)  20.1 us
    ppermute x4, waiting for transfers between devices, with_halo(): lax.ppermute(lax.slice_in_dim(block, 0, width, axis=dim), axis, backward)  13.8 us
    dot_general x2, matrix products, deflate(): jnp.dot(vectors.reshape(number, -1), stacked.reshape(-1, stacked.shape[-1...  7.76 us
    dot_general x2, matrix products, deflate(): jnp.einsum('ktzyxci,ckn->tzyxin', halves, dstack, precision=lax.Precision...  7.2 us
  transfers between devices with their start and end apart: 12, of which 7 were waited for; matrix products, arithmetic and copies ran while one was open for 13% of the time, Pallas kernels for 0%

commit v1 on v0

v1 whole, which is shorter than its diff:
```python
import functools

import jax
import jax.numpy as jnp
from jax import lax
from jax.experimental import pallas as pl
from jax.experimental.pallas import tpu as pltpu
from jax.sharding import PartitionSpec as P

ITERS = 2
MESH = pl.DeviceIdType.MESH
F32 = jnp.float32
BF16 = jnp.bfloat16


def split(value):
    high = value.astype(BF16)
    low = (value - high.astype(F32)).astype(BF16)
    return high, low


def times_i(v):
    middle = v.shape[-1] // 2
    return jnp.concatenate([-v[:, middle:], v[:, :middle]], axis=1)


def times_minus_i(v):
    middle = v.shape[-1] // 2
    return jnp.concatenate([v[:, middle:], -v[:, :middle]], axis=1)


def dot(a, b):
    return jnp.dot(a, b, preferred_element_type=F32)


class Dims:
    def __init__(self, mesh, ly, lx, nc, width, nv):
        self.ns, self.nt = mesh.shape["space"], mesh.shape["tm"]
        self.ly, self.lx, self.nc, self.width, self.nv = ly, lx, nc, width, nv
        self.sites = ly * lx
        self.members = self.ns // 2 * self.nt
        self.half = nv // 2
        self.pieces = min(self.members, self.half // 8)
        self.rows = self.half // self.pieces


def kernel(
    D, coup_h, src_h, x0_h, vec_h, eig, sol, res,
    coup, src, x0, vec, x1, local_sem,
    m_self, m_halo, wk_hi, wk_lo, wt_hi, wt_lo, acc, dst_hi, dst_lo,
    halo, part, core_in, mine, rs_in, dfull,
    halo_send, halo_recv, core_send, core_recv, rs_send, rs_recv, ag_send, ag_recv, re_send, re_recv,
):
    ns, nt, sites, nc, lx, ly = D.ns, D.nt, D.sites, D.nc, D.lx, D.ly
    nv, half, rows, pieces, members = D.nv, D.half, D.rows, D.pieces, D.members
    me_s, me_t = lax.axis_index("space"), lax.axis_index("tm")
    parity = lax.rem(me_s, 2)
    pairs = ns // 2
    rank = me_t * pairs + me_s // 2
    partner = {"space": me_s + 1 - 2 * parity, "tm": me_t}

    loads = [
        pltpu.make_async_copy(x0_h, x0, local_sem.at[0]),
        pltpu.make_async_copy(coup_h, coup, local_sem.at[1]),
        pltpu.make_async_copy(vec_h, vec, local_sem.at[2]),
        pltpu.make_async_copy(src_h, src, local_sem.at[3]),
    ]
    for load in loads:
        load.start()

    barrier = pltpu.get_barrier_semaphore()
    total = ns * nt
    flat = me_t * ns + me_s

    def greet(o, carry):
        other = lax.rem(flat + o, total)
        pl.semaphore_signal(
            barrier, inc=1, device_id={"space": lax.rem(other, ns), "tm": other // ns}, device_id_type=MESH
        )
        return carry

    lax.fori_loop(1, total, greet, 0)
    pl.semaphore_wait(barrier, total - 1)

    up_s, down_s = lax.rem(me_s + 1, ns), lax.rem(me_s + ns - 1, ns)
    up_t, down_t = lax.rem(me_t + 1, nt), lax.rem(me_t + nt - 1, nt)
    targets = (
        (2, {"space": me_s, "tm": down_t}),
        (3, {"space": me_s, "tm": up_t}),
        (0, {"space": down_s, "tm": me_t}),
        (1, {"space": up_s, "tm": me_t}),
    )

    def halo_copy(it, site, slot, target):
        source = x0_h if it == 0 else x1
        return pltpu.make_async_remote_copy(
            src_ref=source.at[site],
            dst_ref=halo.at[it, slot, site],
            send_sem=halo_send.at[it, slot, site],
            recv_sem=halo_recv.at[it, slot, site],
            device_id=target,
            device_id_type=MESH,
        )

    def send_halo(it, first, count):
        def body(site, carry):
            for slot, target in targets:
                halo_copy(it, site, slot, target).start()
            return carry

        lax.fori_loop(first, first + count, body, 0)

    send_halo(0, 0, sites)
    sign_up = jnp.where(me_t == nt - 1, -1.0, 1.0).astype(F32)
    sign_down = jnp.where(me_t == 0, -1.0, 1.0).astype(F32)

    for load in loads:
        load.wait()

    def outs_of(site):
        y, x = site // lx, lax.rem(site, lx)
        return (
            site,
            y * lx + lax.rem(x + lx - 1, lx),
            y * lx + lax.rem(x + 1, lx),
            lax.rem(y + ly - 1, ly) * lx + x,
            lax.rem(y + 1, ly) * lx + x,
        )

    def prepare_matrices(site, carry):
        for d, out in enumerate(outs_of(site)):
            high, low = split(coup[d, out])
            m_self[site, d * nc:(d + 1) * nc, :] = high
            m_self[site, (5 + d) * nc:(6 + d) * nc, :] = low
        for d in range(4):
            high, low = split(coup[5 + d, site])
            m_halo[d, site, 0:nc, :] = high
            m_halo[d, site, nc:2 * nc, :] = low
        return carry

    lax.fori_loop(0, sites, prepare_matrices, 0)

    def stacked(value):
        high, low = split(value)
        return (
            jnp.concatenate([high, times_i(high)], axis=0),
            jnp.concatenate([low, times_i(low)], axis=0),
        )

    def self_part(field):
        acc[...] = jnp.zeros_like(acc)

        def body(site, carry):
            high, low = stacked(field[site])
            one = dot(m_self[site], high)
            two = dot(m_self[site, 0:5 * nc, :], low)
            for d, out in enumerate(outs_of(site)):
                acc[out] += (
                    one[d * nc:(d + 1) * nc] + one[(5 + d) * nc:(6 + d) * nc] + two[d * nc:(d + 1) * nc]
                )
            return carry

        lax.fori_loop(0, sites, body, 0)

    def prepare_vectors(site, carry):
        w = vec[site]
        high, low = split(w)
        wk_hi[site] = high
        wk_lo[site] = low
        turned = w.T
        high, low = split(turned)
        wt_hi[site, :, 0:nv] = high[0:nc]
        wt_hi[site, :, nv:2 * nv] = high[nc:2 * nc]
        wt_lo[site, :, 0:nv] = low[0:nc]
        wt_lo[site, :, nv:2 * nv] = low[nc:2 * nc]
        return carry

    def halo_part(it, out):
        def body(site, carry):
            total = acc[site]
            for slot, sign in ((0, None), (1, None), (2, sign_up), (3, sign_down)):
                copy = [t for t in targets if t[0] == slot][0]
                halo_copy(it, site, slot, copy[1]).wait_recv()
                value = halo[it, slot, site]
                if sign is not None:
                    value = value * sign
                high, low = stacked(value)
                one = dot(m_halo[slot, site], high)
                two = dot(m_halo[slot, site, 0:nc, :], low)
                total = total + (one[0:nc] + one[nc:2 * nc] + two)
            residual = src[site] - total
            out[site] = residual
            high, low = split(residual)
            high = jnp.concatenate([high, times_minus_i(high)], axis=0)
            low = jnp.concatenate([low, times_minus_i(low)], axis=0)
            part[it] += dot(wk_hi[site], high) + dot(wk_hi[site], low) + dot(wk_lo[site], high)
            return carry

        part[it] = jnp.zeros((nv, D.width), F32)
        lax.fori_loop(0, sites, body, 0)

    def member(q):
        return {"space": lax.rem(q, pairs) * 2 + parity, "tm": q // pairs}

    my_rows = pl.multiple_of(parity * half, 8)
    other_rows = pl.multiple_of((1 - parity) * half, 8)
    piece = lax.rem(rank, pieces)
    block = rank - piece
    piece_row = pl.multiple_of(my_rows + piece * rows, 8)

    def core_copy(it):
        return pltpu.make_async_remote_copy(
            src_ref=part.at[it, pl.ds(other_rows, half)],
            dst_ref=core_in.at[it],
            send_sem=core_send.at[it],
            recv_sem=core_recv.at[it],
            device_id=partner,
            device_id_type=MESH,
        )

    def rs_copy(it, o):
        q = lax.rem(rank + o, members)
        row = pl.multiple_of(lax.rem(q, pieces) * rows, 8)
        return pltpu.make_async_remote_copy(
            src_ref=mine.at[it, pl.ds(row, rows)],
            dst_ref=rs_in.at[it, o],
            send_sem=rs_send.at[it, o],
            recv_sem=rs_recv.at[it, o],
            device_id=member(q),
            device_id_type=MESH,
        )

    def ag_copy(it, o):
        q = block + lax.rem(piece + o, pieces)
        return pltpu.make_async_remote_copy(
            src_ref=dfull.at[it, pl.ds(piece_row, rows)],
            dst_ref=dfull.at[it, pl.ds(piece_row, rows)],
            send_sem=ag_send.at[it, o],
            recv_sem=ag_recv.at[it, o],
            device_id=member(q),
            device_id_type=MESH,
        )

    def relay_copy(it, o):
        row = pl.multiple_of(my_rows + lax.rem(piece + pieces - o, pieces) * rows, 8)
        return pltpu.make_async_remote_copy(
            src_ref=dfull.at[it, pl.ds(row, rows)],
            dst_ref=dfull.at[it, pl.ds(row, rows)],
            send_sem=re_send.at[it, o],
            recv_sem=re_recv.at[it, o],
            device_id=partner,
            device_id_type=MESH,
        )

    def loop(start, stop, action):
        def body(o, carry):
            action(o)
            return carry

        lax.fori_loop(start, stop, body, 0)

    def reduce_coefficients(it):
        core_copy(it).start()
        core_copy(it).wait_recv()
        mine[it] = part[it, pl.ds(my_rows, half), :] + core_in[it]
        loop(1, members, lambda o: rs_copy(it, o).start())
        own = mine[it, pl.ds(pl.multiple_of(piece * rows, 8), rows), :]

        def gather(o, total):
            rs_copy(it, o).wait_recv()
            return total + rs_in[it, o]

        coef = lax.fori_loop(1, members, gather, own)
        eigen = eig[pl.ds(piece_row, rows), :]
        dfull[it, pl.ds(piece_row, rows), :] = eigen[:, 0:1] * coef + eigen[:, 1:2] * times_i(coef)
        loop(1, pieces, lambda o: ag_copy(it, o).start())
        relay_copy(it, 0).start()

        def forward(o):
            ag_copy(it, o).wait_recv()
            relay_copy(it, o).start()

        loop(1, pieces, forward)
        loop(0, pieces, lambda o: relay_copy(it, o).wait_recv())
        high, low = split(dfull[it])
        dst_hi[0:nv, :] = high
        dst_hi[nv:2 * nv, :] = times_i(high)
        dst_lo[0:nv, :] = low
        dst_lo[nv:2 * nv, :] = times_i(low)

    def update(it, old, residual, out, group):
        def body(g, carry):
            first = g * group
            a_hi = wt_hi[pl.ds(first, group)].reshape(group * nc, 2 * nv)
            a_lo = wt_lo[pl.ds(first, group)].reshape(group * nc, 2 * nv)
            deflated = dot(a_hi, dst_hi[...]) + dot(a_hi, dst_lo[...]) + dot(a_lo, dst_hi[...])
            deflated = deflated.reshape(group, nc, D.width)
            now = pl.ds(first, group)
            out[now] = old[now] + deflated + 0.5 * residual[now]
            if it + 1 < ITERS:
                send_halo(it + 1, first, group)
            return carry

        lax.fori_loop(0, sites // group, body, 0)

    group = 4 if sites % 4 == 0 else 1
    self_part(x0)
    lax.fori_loop(0, sites, prepare_vectors, 0)
    halo_part(0, res)
    reduce_coefficients(0)
    update(0, x0, res, x1, group)
    self_part(x1)
    halo_part(1, res)
    reduce_coefficients(1)
    update(1, x1, res, sol, group)

    for it in range(ITERS):
        core_copy(it).wait_send()
        loop(1, members, lambda o: rs_copy(it, o).wait_send())
        loop(1, pieces, lambda o: ag_copy(it, o).wait_send())
        loop(0, pieces, lambda o: relay_copy(it, o).wait_send())

        def drain(site):
            for slot, target in targets:
                halo_copy(it, site, slot, target).wait_send()

        loop(0, sites, drain)


def solve(mesh, couplings, source, initial, vectors, inverse_eigen):
    nine, _, _, ly, lx, nc, _ = couplings.shape
    width = source.shape[-1]
    nv = vectors.shape[0]
    D = Dims(mesh, ly, lx, nc, width, nv)
    sites = D.sites
    field = (sites, nc, width)
    vecs = vectors.reshape(nv, sites, 2 * nc).transpose(1, 0, 2)
    any_spec = pl.BlockSpec(memory_space=pl.ANY)
    vmem = pl.BlockSpec(memory_space=pltpu.VMEM)
    dma = pltpu.SemaphoreType.DMA
    out = jax.ShapeDtypeStruct(field, F32)
    x, r = pl.pallas_call(
        functools.partial(kernel, D),
        out_shape=(out, out),
        in_specs=[any_spec, any_spec, any_spec, any_spec, vmem],
        out_specs=(vmem, vmem),
        scratch_shapes=[
            pltpu.VMEM((nine, sites, nc, 2 * nc), F32),
            pltpu.VMEM(field, F32),
            pltpu.VMEM(field, F32),
            pltpu.VMEM((sites, nv, 2 * nc), F32),
            pltpu.VMEM(field, F32),
            dma((4,)),
            pltpu.VMEM((sites, 10 * nc, 2 * nc), BF16),
            pltpu.VMEM((4, sites, 2 * nc, 2 * nc), BF16),
            pltpu.VMEM((sites, nv, 2 * nc), BF16),
            pltpu.VMEM((sites, nv, 2 * nc), BF16),
            pltpu.VMEM((sites, nc, 2 * nv), BF16),
            pltpu.VMEM((sites, nc, 2 * nv), BF16),
            pltpu.VMEM(field, F32),
            pltpu.VMEM((2 * nv, width), BF16),
            pltpu.VMEM((2 * nv, width), BF16),
            pltpu.VMEM((ITERS, 4) + field, F32),
            pltpu.VMEM((ITERS, nv, width), F32),
            pltpu.VMEM((ITERS, D.half, width), F32),
            pltpu.VMEM((ITERS, D.half, width), F32),
            pltpu.VMEM((ITERS, D.members, D.rows, width), F32),
            pltpu.VMEM((ITERS, nv, width), F32),
            dma((ITERS, 4, sites)),
            dma((ITERS, 4, sites)),
            dma((ITERS,)),
            dma((ITERS,)),
            dma((ITERS, D.members)),
            dma((ITERS, D.members)),
            dma((ITERS, D.pieces)),
            dma((ITERS, D.pieces)),
            dma((ITERS, D.pieces)),
            dma((ITERS, D.pieces)),
        ],
        compiler_params=pltpu.CompilerParams(
            collective_id=0, has_side_effects=True, vmem_limit_bytes=60 * 1024 * 1024
        ),
    )(
        couplings.reshape(nine, sites, nc, 2 * nc),
        source.reshape(field),
        initial.reshape(field),
        vecs,
        inverse_eigen.T,
    )
    return x.reshape(source.shape), r.reshape(source.shape)


def solution(mesh):
    in_specs = (
        P(None, "tm", "space", None, None, None, None),
        P("tm", "space", None, None, None, None),
        P("tm", "space", None, None, None, None),
        P(None, "tm", "space", None, None, None),
        P(),
    )
    out_specs = (
        P(("groups", "tm"), "space", None, None, None, None),
        P(("groups", "tm"), "space", None, None, None, None),
    )
    return jax.shard_map(
        functools.partial(solve, mesh), mesh=mesh, in_specs=in_specs, out_specs=out_specs, check_vma=False
    )
```

time: 264 us -> 131 us (0.50)
  waiting for transfers between devices: 156 us -> 0 us
  Pallas kernels: 0 us -> 119 us
  matrix products: 48.7 us -> 0 us
  blocking collectives: 20.1 us -> 0 us
  between operations: 14.4 us -> 0.64 us
  other arithmetic: 9.61 us -> 0 us
  starting transfers between devices: 9.09 us -> 0 us
  local copies, waits for them, and re-layouts: 4.8 us -> 10.6 us
    pallas_call x0 -> x1, Pallas kernels: none -> 119 us  [solve(): pl.pallas_call(functools.partial(kernel, D), out_shape=(out, out), in_spe...]
    psum x2 -> x0, waiting for transfers between devices: 69.8 us -> none  [deflate(): over_time = lax.psum(partial_value, 'tm')]
    dot_general x22 -> x0, matrix products: 48.7 us -> none  [the longest x18 33.7 us: coupled(): jnp.einsum('tzyxij,tzyxjn->tzyxin', matrix, stacked, precision=lax.Precis...]
    ppermute x8 -> x0, waiting for transfers between devices: 44.4 us -> none  [the longest x4 30.5 us: with_halo(): lax.ppermute(lax.slice_in_dim(block, block.shape[dim] - width, None, axis...]
    reduce_scatter x2 -> x0, waiting for transfers between devices: 41.9 us -> none  [deflate(): lax.psum_scatter(over_time, 'space', scatter_dimension=0, tiled=True)]
    all_gather x2 -> x0, blocking collectives: 20.1 us -> none  [deflate(): lax.all_gather(scale_coeffs(owned, eigen_part), 'space', axis=0, tiled=True)]
    ppermute x8 -> x0, starting transfers between devices: 8.93 us -> none  [the longest x4 6.23 us: with_halo(): lax.ppermute(lax.slice_in_dim(block, 0, width, axis=dim), axis, backward)]
    unnamed x34 -> x4, local copies, waits for them, and re-layouts: 1.82 us -> 10.6 us
  transfers between devices with their start and end apart: 12 -> 0, of which waited for: 7 -> 0; matrix products, arithmetic and copies ran while one was open for 13% -> 0% of each run, Pallas kernels for 0% -> 0%
where the time goes in v1:
time: 131 us; the launch traced here: 130 us
  Pallas kernels  119 us (91%)
  local copies, waits for them, and re-layouts  10.6 us (8%)
    pallas_call x1, Pallas kernels, solve(): pl.pallas_call(functools.partial(kernel, D), out_shape=(out, out), in_spe...  119 us
    unnamed x4, local copies, waits for them, and re-layouts  10.6 us

profile of v1, /device:TPU:1, one launch (start us, length us, event | category | flops | bytes accessed | tf_op | source)
XLA Modules:
  0.0 130.4 jit_solution(16692585509755019706)
XLA Ops:
  0.6 1.5 %copy.8 = f32[2,512]{0,1:T(8,128)} copy(f32[2,512]{1,0:T(2,128)} %param.9) | data formatting | bytes 8192 | tf_op args[4]
  2.2 5.0 %copy.7 = f32[512,1,1,2,4,192]{5,0,4,3,2,1:T(8,128)} copy(f32[512,1,1,2,4,192]{0,5,4,3,2,1:T(8,128)} %param.8) | data formatting | bytes 6291456 | tf_op args[3]
  7.1 119.1 %shard_map.68 = (f32[8,96,256]{2,1,0:T(8,128)}, f32[8,96,256]{2,1,0:T(8,128)}) custom-call(f32[9,8,96,192]{3,2,1,0:T(8,128)} %bitcast.10, f32[8,96,256]{2,1,0:T(8,128)} %bitcast.12, f32[8,96,256]{2,1,0:T(8,128)} %bitcast.13, f32[8,512,192]{2,1,0:T(8,128)} %bitcast.9, f32[512,2]{1,0:T(8,128)} %bitcast.11), custom_call_target="tpu_custom_call" | custom-call | tf_op jit(solution)/shard_map/pallas_call | solution.py:342
  126.2 2.1 %copy.11 = f32[1,1,2,4,96,256]{5,4,3,2,1,0:T(8,128)} copy(f32[1,1,2,4,96,256]{5,4,3,2,1,0:T(8,128)} %bitcast.15) | data formatting | bytes 1572864
  128.3 2.1 %copy.12 = f32[1,1,2,4,96,256]{5,4,3,2,1,0:T(8,128)} copy(f32[1,1,2,4,96,256]{5,4,3,2,1,0:T(8,128)} %bitcast.14) | data formatting | bytes 1572864

commit v2 on v1

v2 whole, which is shorter than its diff:
```python
import functools

import jax
import jax.numpy as jnp
from jax import lax
from jax.experimental import pallas as pl
from jax.experimental.pallas import tpu as pltpu
from jax.sharding import PartitionSpec as P

ITERS = 2
MESH = pl.DeviceIdType.MESH
F32 = jnp.float32
BF16 = jnp.bfloat16


def split(value):
    high = value.astype(BF16)
    low = (value - high.astype(F32)).astype(BF16)
    return high, low


def turn(v):
    middle = v.shape[-1] // 2
    lane = lax.broadcasted_iota(jnp.int32, v.shape, 1)
    return jnp.where(lane < middle, -1.0, 1.0) * pltpu.roll(v, middle, 1)


def dot(a, b):
    return jnp.dot(a, b, preferred_element_type=F32)


AHEAD = 3


class Dims:
    def __init__(self, mesh, ly, lx, nc, width, nv):
        self.ns, self.nt = mesh.shape["space"], mesh.shape["tm"]
        self.ly, self.lx, self.nc, self.width, self.nv = ly, lx, nc, width, nv
        self.chunks = 2
        self.cw = width // self.chunks
        self.phases = ITERS * self.chunks
        self.sites = ly * lx
        self.members = self.ns // 2 * self.nt
        self.half = nv // 2
        self.pieces = min(self.members, self.half // 8)
        self.rows = self.half // self.pieces


def kernel(
    D, coup_h, src_in, x0_in, vec_h, eig, sol, res_out,
    coup, vec, x0, src, x1, xf, res, local_sem,
    m_self, m_halo, wk_hi, wk_lo, wt_hi, wt_lo, acc, dst_hi, dst_lo,
    halo, part, core_in, mine, rs_in, dfull, eig_t,
    halo_send, halo_recv, core_send, core_recv, rs_send, rs_recv, ag_send, ag_recv, re_send, re_recv,
):
    ns, nt, sites, nc, lx, ly = D.ns, D.nt, D.sites, D.nc, D.lx, D.ly
    nv, half, rows, pieces, members = D.nv, D.half, D.rows, D.pieces, D.members
    chunks, cw, width = D.chunks, D.cw, D.width
    me_s, me_t = lax.axis_index("space"), lax.axis_index("tm")
    parity = lax.rem(me_s, 2)
    pairs = ns // 2
    rank = me_t * pairs + me_s // 2
    partner = {"space": me_s + 1 - 2 * parity, "tm": me_t}

    def loop(start, stop, action):
        def body(o, carry):
            action(o)
            return carry

        lax.fori_loop(start, stop, body, 0)

    loads = [
        pltpu.make_async_copy(coup_h, coup, local_sem.at[0]),
        pltpu.make_async_copy(vec_h, vec, local_sem.at[1]),
    ]
    for load in loads:
        load.start()

    barrier = pltpu.get_barrier_semaphore()
    total = ns * nt
    flat = me_t * ns + me_s

    def greet(o):
        other = lax.rem(flat + o, total)
        pl.semaphore_signal(
            barrier, inc=1, device_id={"space": lax.rem(other, ns), "tm": other // ns}, device_id_type=MESH
        )

    loop(1, total, greet)

    def pack(whole, parts):
        def body(site):
            value = whole[site]
            h, middle = cw // 2, width // 2
            for g in range(chunks):
                parts[g, site] = jnp.concatenate(
                    [value[:, g * h:(g + 1) * h], value[:, middle + g * h:middle + (g + 1) * h]], axis=1
                )

        loop(0, sites, body)

    def unpack(parts, whole):
        def body(site):
            h = cw // 2
            values = [parts[g, site] for g in range(chunks)]
            whole[site] = jnp.concatenate([v[:, :h] for v in values] + [v[:, h:] for v in values], axis=1)

        loop(0, sites, body)

    pack(x0_in, x0)
    pl.semaphore_wait(barrier, total - 1)

    up_s, down_s = lax.rem(me_s + 1, ns), lax.rem(me_s + ns - 1, ns)
    up_t, down_t = lax.rem(me_t + 1, nt), lax.rem(me_t + nt - 1, nt)
    targets = (
        (2, {"space": me_s, "tm": down_t}),
        (3, {"space": me_s, "tm": up_t}),
        (0, {"space": down_s, "tm": me_t}),
        (1, {"space": up_s, "tm": me_t}),
    )
    target_of = dict(targets)

    def field_of(p):
        return (x0 if p < chunks else x1).at[p % chunks]

    def halo_copy(p, site, slot):
        return pltpu.make_async_remote_copy(
            src_ref=field_of(p).at[site],
            dst_ref=halo.at[p, slot, site],
            send_sem=halo_send.at[p, slot, site],
            recv_sem=halo_recv.at[p, slot, site],
            device_id=target_of[slot],
            device_id_type=MESH,
        )

    def send_site(p, site):
        for slot, _ in targets:
            halo_copy(p, site, slot).start()

    loop(0, sites, lambda site: send_site(0, site))
    sign_up = jnp.where(me_t == nt - 1, -1.0, 1.0).astype(F32)
    sign_down = jnp.where(me_t == 0, -1.0, 1.0).astype(F32)

    pack(src_in, src)
    eig_t[...] = jnp.concatenate([eig[...]] * 4, axis=0).T
    for load in loads:
        load.wait()

    def outs_of(site):
        y, x = site // lx, lax.rem(site, lx)
        return (
            site,
            y * lx + lax.rem(x + lx - 1, lx),
            y * lx + lax.rem(x + 1, lx),
            lax.rem(y + ly - 1, ly) * lx + x,
            lax.rem(y + 1, ly) * lx + x,
        )

    def prepare_matrices(site):
        for d, out in enumerate(outs_of(site)):
            high, low = split(coup[d, out])
            m_self[site, d * nc:(d + 1) * nc, :] = high
            m_self[site, (5 + d) * nc:(6 + d) * nc, :] = low
        for d in range(4):
            high, low = split(coup[5 + d, site])
            m_halo[d, site, 0:nc, :] = high
            m_halo[d, site, nc:2 * nc, :] = low

    def prepare_vectors(site):
        turned = vec[site]
        high, low = split(turned.T)
        wk_hi[site] = high
        wk_lo[site] = low
        high, low = split(turned)
        wt_hi[site, :, 0:nv] = high[0:nc]
        wt_hi[site, :, nv:2 * nv] = high[nc:2 * nc]
        wt_lo[site, :, 0:nv] = low[0:nc]
        wt_lo[site, :, nv:2 * nv] = low[nc:2 * nc]

    def stacked(value, other):
        high, low = split(value)
        other_high, other_low = split(other)
        return jnp.concatenate([high, other_high], axis=0), jnp.concatenate([low, other_low], axis=0)

    def self_part(p):
        acc[...] = jnp.zeros_like(acc)
        field = field_of(p)

        def body(site):
            value = field[site]
            high, low = stacked(value, turn(value))
            one = dot(m_self[site], high)
            two = dot(m_self[site, 0:5 * nc, :], low)
            for d, out in enumerate(outs_of(site)):
                acc[out] += (
                    one[d * nc:(d + 1) * nc] + one[(5 + d) * nc:(6 + d) * nc] + two[d * nc:(d + 1) * nc]
                )

        loop(0, sites, body)
        part[p] = jnp.zeros((nv, cw), F32)

    def halo_site(p, site):
        g = p % chunks
        total = acc[site]
        for slot, sign in ((0, None), (1, None), (2, sign_up), (3, sign_down)):
            halo_copy(p, site, slot).wait_recv()
            value = halo[p, slot, site]
            if sign is not None:
                value = value * sign
            high, low = stacked(value, turn(value))
            one = dot(m_halo[slot, site], high)
            two = dot(m_halo[slot, site, 0:nc, :], low)
            total = total + (one[0:nc] + one[nc:2 * nc] + two)
        residual = src[g, site] - total
        res[g, site] = residual
        high, low = stacked(residual, -turn(residual))
        part[p] += dot(wk_hi[site], high) + dot(wk_hi[site], low) + dot(wk_lo[site], high)
        if p == 0:
            ahead = site + AHEAD - sites

            @pl.when(ahead >= 0)
            def _():
                send_site(1, ahead)
        else:
            @pl.when(site + AHEAD < sites)
            def _():
                send_site(p, site + AHEAD)

    def member(q):
        return {"space": lax.rem(q, pairs) * 2 + parity, "tm": q // pairs}

    my_rows = pl.multiple_of(parity * half, 8)
    other_rows = pl.multiple_of((1 - parity) * half, 8)
    piece = lax.rem(rank, pieces)
    block = rank - piece
    piece_row = pl.multiple_of(my_rows + piece * rows, 8)

    def core_copy(p):
        return pltpu.make_async_remote_copy(
            src_ref=part.at[p, pl.ds(other_rows, half)],
            dst_ref=core_in.at[p],
            send_sem=core_send.at[p],
            recv_sem=core_recv.at[p],
            device_id=partner,
            device_id_type=MESH,
        )

    def rs_copy(p, o):
        q = lax.rem(rank + o, members)
        row = pl.multiple_of(lax.rem(q, pieces) * rows, 8)
        return pltpu.make_async_remote_copy(
            src_ref=mine.at[p, pl.ds(row, rows)],
            dst_ref=rs_in.at[p, o],
            send_sem=rs_send.at[p, o],
            recv_sem=rs_recv.at[p, o],
            device_id=member(q),
            device_id_type=MESH,
        )

    def ag_copy(p, o):
        q = block + lax.rem(piece + o, pieces)
        return pltpu.make_async_remote_copy(
            src_ref=dfull.at[p, pl.ds(piece_row, rows)],
            dst_ref=dfull.at[p, pl.ds(piece_row, rows)],
            send_sem=ag_send.at[p, o],
            recv_sem=ag_recv.at[p, o],
            device_id=member(q),
            device_id_type=MESH,
        )

    def relay_copy(p, o):
        row = pl.multiple_of(my_rows + lax.rem(piece + pieces - o, pieces) * rows, 8)
        return pltpu.make_async_remote_copy(
            src_ref=dfull.at[p, pl.ds(row, rows)],
            dst_ref=dfull.at[p, pl.ds(row, rows)],
            send_sem=re_send.at[p, o],
            recv_sem=re_recv.at[p, o],
            device_id=partner,
            device_id_type=MESH,
        )

    def reduce_start(p):
        core_copy(p).wait_recv()
        mine[p] = part[p, pl.ds(my_rows, half), :] + core_in[p]
        loop(1, members, lambda o: rs_copy(p, o).start())

    def gather_start(p):
        own = mine[p, pl.ds(pl.multiple_of(piece * rows, 8), rows), :]

        def gather(o, total):
            rs_copy(p, o).wait_recv()
            return total + rs_in[p, o]

        coef = lax.fori_loop(1, members, gather, own)
        eigen = eig_t[pl.ds(piece_row, rows), :]
        dfull[p, pl.ds(piece_row, rows), :] = eigen[:, 0:1] * coef + eigen[:, 1:2] * turn(coef)
        loop(1, pieces, lambda o: ag_copy(p, o).start())
        relay_copy(p, 0).start()

    def forward(p):
        def action(o):
            ag_copy(p, o).wait_recv()
            relay_copy(p, o).start()

        loop(1, pieces, action)

    def update(p):
        loop(0, pieces, lambda o: relay_copy(p, o).wait_recv())
        d = dfull[p]
        high, low = stacked(d, turn(d))
        dst_hi[...] = high
        dst_lo[...] = low
        g, later = p % chunks, p + chunks
        old, new = (x0, x1) if p < chunks else (x1, xf)
        group = 4 if sites % 4 == 0 else 1

        def body(b):
            first = b * group
            a_hi = wt_hi[pl.ds(first, group)].reshape(group * nc, 2 * nv)
            a_lo = wt_lo[pl.ds(first, group)].reshape(group * nc, 2 * nv)
            deflated = dot(a_hi, dst_hi[...]) + dot(a_hi, dst_lo[...]) + dot(a_lo, dst_hi[...])
            deflated = deflated.reshape(group, nc, cw)
            now = pl.ds(first, group)
            new[g, now] = old[g, now] + deflated + 0.5 * res[g, now]
            if later < D.phases:
                @pl.when(b == 0)
                def _():
                    for site in range(AHEAD):
                        send_site(later, site)

        loop(0, sites // group, body)

    loop(0, sites, prepare_matrices)
    self_part(0)
    loop(0, sites, prepare_vectors)
    loop(0, sites, lambda site: halo_site(0, site))
    core_copy(0).start()
    cuts = (0, sites // 8, sites // 2, sites - sites // 8, sites)
    for p in range(1, D.phases):
        self_part(p)
        stages = (reduce_start, gather_start, forward, None)
        for stage, start, stop in zip(stages, cuts[:-1], cuts[1:]):
            loop(start, stop, lambda site: halo_site(p, site))
            if stage is not None:
                stage(p - 1)
            if stage is forward:
                update(p - 1)
        core_copy(p).start()
    last = D.phases - 1
    unpack(res, res_out)
    reduce_start(last)
    gather_start(last)
    forward(last)
    update(last)
    unpack(xf, sol)

    for p in range(D.phases):
        core_copy(p).wait_send()
        loop(1, members, lambda o: rs_copy(p, o).wait_send())
        loop(1, pieces, lambda o: ag_copy(p, o).wait_send())
        loop(0, pieces, lambda o: relay_copy(p, o).wait_send())

        def drain(site):
            for slot, _ in targets:
                halo_copy(p, site, slot).wait_send()

        loop(0, sites, drain)


def solve(mesh, couplings, source, initial, vectors, inverse_eigen):
    nine, _, _, ly, lx, nc, _ = couplings.shape
    width = source.shape[-1]
    nv = vectors.shape[0]
    D = Dims(mesh, ly, lx, nc, width, nv)
    sites, phases, cw = D.sites, D.phases, D.cw
    field = (sites, nc, width)
    chunked = (D.chunks, sites, nc, cw)
    vecs = vectors.reshape(nv, sites, 2 * nc).transpose(1, 2, 0)
    any_spec = pl.BlockSpec(memory_space=pl.ANY)
    vmem = pl.BlockSpec(memory_space=pltpu.VMEM)
    dma = pltpu.SemaphoreType.DMA
    out = jax.ShapeDtypeStruct(field, F32)
    x, r = pl.pallas_call(
        functools.partial(kernel, D),
        out_shape=(out, out),
        in_specs=[any_spec, vmem, vmem, any_spec, vmem],
        out_specs=(vmem, vmem),
        scratch_shapes=[
            pltpu.VMEM((nine, sites, nc, 2 * nc), F32),
            pltpu.VMEM((sites, 2 * nc, nv), F32),
            pltpu.VMEM(chunked, F32),
            pltpu.VMEM(chunked, F32),
            pltpu.VMEM(chunked, F32),
            pltpu.VMEM(chunked, F32),
            pltpu.VMEM(chunked, F32),
            dma((2,)),
            pltpu.VMEM((sites, 10 * nc, 2 * nc), BF16),
            pltpu.VMEM((4, sites, 2 * nc, 2 * nc), BF16),
            pltpu.VMEM((sites, nv, 2 * nc), BF16),
            pltpu.VMEM((sites, nv, 2 * nc), BF16),
            pltpu.VMEM((sites, nc, 2 * nv), BF16),
            pltpu.VMEM((sites, nc, 2 * nv), BF16),
            pltpu.VMEM((sites, nc, cw), F32),
            pltpu.VMEM((2 * nv, cw), BF16),
            pltpu.VMEM((2 * nv, cw), BF16),
            pltpu.VMEM((phases, 4, sites, nc, cw), F32),
            pltpu.VMEM((phases, nv, cw), F32),
            pltpu.VMEM((phases, D.half, cw), F32),
            pltpu.VMEM((phases, D.half, cw), F32),
            pltpu.VMEM((phases, D.members, D.rows, cw), F32),
            pltpu.VMEM((phases, nv, cw), F32),
            pltpu.VMEM((nv, 8), F32),
            dma((phases, 4, sites)),
            dma((phases, 4, sites)),
            dma((phases,)),
            dma((phases,)),
            dma((phases, D.members)),
            dma((phases, D.members)),
            dma((phases, D.pieces)),
            dma((phases, D.pieces)),
            dma((phases, D.pieces)),
            dma((phases, D.pieces)),
        ],
        compiler_params=pltpu.CompilerParams(
            collective_id=0, has_side_effects=True, vmem_limit_bytes=50000 * 1024
        ),
    )(
        couplings.reshape(nine, sites, nc, 2 * nc),
        source.reshape(field),
        initial.reshape(field),
        vecs,
        inverse_eigen,
    )
    return x.reshape(source.shape), r.reshape(source.shape)


def solution(mesh):
    in_specs = (
        P(None, "tm", "space", None, None, None, None),
        P("tm", "space", None, None, None, None),
        P("tm", "space", None, None, None, None),
        P(None, "tm", "space", None, None, None),
        P(),
    )
    out_specs = (
        P(("groups", "tm"), "space", None, None, None, None),
        P(("groups", "tm"), "space", None, None, None, None),
    )
    return jax.shard_map(
        functools.partial(solve, mesh), mesh=mesh, in_specs=in_specs, out_specs=out_specs, check_vma=False
    )
```

time: 131 us -> 127 us (0.969)
  local copies, waits for them, and re-layouts: 10.6 us -> 4.71 us
  Pallas kernels: 119 us -> 121 us
    unnamed x4 -> x8, local copies, waits for them, and re-layouts: 10.6 us -> 4.71 us
    pallas_call x1, Pallas kernels: 119 us -> 121 us  [solve(): pl.pallas_call(functools.partial(kernel, D), out_shape=(out, out), in_spe...]
where the time goes in v2:
time: 127 us
  Pallas kernels  121 us (95%)
  local copies, waits for them, and re-layouts  4.71 us (4%)
    pallas_call x1, Pallas kernels, solve(): pl.pallas_call(functools.partial(kernel, D), out_shape=(out, out), in_spe...  121 us
    unnamed x8, local copies, waits for them, and re-layouts  4.71 us

profile of v2, /device:TPU:1, one launch (start us, length us, event | category | flops | bytes accessed | tf_op | source)
XLA Modules:
  0.0 126.8 jit_solution(9031051244036925523)
XLA Ops:
  0.6 0.0 copy-start
  0.6 1.1 copy-done
  1.8 0.0 copy-start.1
  1.8 1.1 copy-done.1
  2.9 0.0 copy-start.2
  2.9 0.7 copy-done.2
  3.6 121.5 %shard_map.68 = (f32[8,96,256]{2,1,0:T(8,128)S(1)}, f32[8,96,256]{2,1,0:T(8,128)S(1)}) custom-call(f32[9,8,96,192]{3,2,1,0:T(8,128)} %bitcast.12, f32[8,96,256]{2,1,0:T(8,128)S(1)} %bitcast.10, f32[8,96,256]{2,1,0:T(8,128)S(1)} %bitcast.11, f32[8,192,512]{2,1,0:T(8,128)} %bitcast.13, f32[2,512]{1,0:T(2,128)S(1)} %copy-done.2), custom_call_target="tpu_custom_call" | custom-call | tf_op jit(solution)/shard_map/pallas_call | solution.py:383
  125.1 0.9 copy.9
  126.0 0.9 copy.10
Async XLA Ops:
  0.6 1.1 copy-start
  1.8 1.1 copy-start.1
  2.9 0.7 copy-start.2

commit v3 on v1

--- a/solution.py
+++ b/solution.py
@@ -48,7 +48,7 @@
     D, coup_h, src_h, x0_h, vec_h, eig, sol, res,
     coup, src, x0, vec, x1, local_sem,
     m_self, m_halo, wk_hi, wk_lo, wt_hi, wt_lo, acc, dst_hi, dst_lo,
-    halo, part, core_in, mine, rs_in, dfull,
+    halo, part, core_in, mine, rs_in, dfull, eig_t,
     halo_send, halo_recv, core_send, core_recv, rs_send, rs_recv, ag_send, ag_recv, re_send, re_recv,
 ):
     ns, nt, sites, nc, lx, ly = D.ns, D.nt, D.sites, D.nc, D.lx, D.ly
@@ -163,11 +163,10 @@
         lax.fori_loop(0, sites, body, 0)
 
     def prepare_vectors(site, carry):
-        w = vec[site]
-        high, low = split(w)
+        turned = vec[site]
+        high, low = split(turned.T)
         wk_hi[site] = high
         wk_lo[site] = low
-        turned = w.T
         high, low = split(turned)
         wt_hi[site, :, 0:nv] = high[0:nc]
         wt_hi[site, :, nv:2 * nv] = high[nc:2 * nc]
@@ -271,7 +270,7 @@
             return total + rs_in[it, o]
 
         coef = lax.fori_loop(1, members, gather, own)
-        eigen = eig[pl.ds(piece_row, rows), :]
+        eigen = eig_t[pl.ds(piece_row, rows), :]
         dfull[it, pl.ds(piece_row, rows), :] = eigen[:, 0:1] * coef + eigen[:, 1:2] * times_i(coef)
         loop(1, pieces, lambda o: ag_copy(it, o).start())
         relay_copy(it, 0).start()
@@ -306,6 +305,7 @@
     group = 4 if sites % 4 == 0 else 1
     self_part(x0)
     lax.fori_loop(0, sites, prepare_vectors, 0)
+    eig_t[...] = jnp.concatenate([eig[...]] * 4, axis=0).T
     halo_part(0, res)
     reduce_coefficients(0)
     update(0, x0, res, x1, group)
@@ -334,7 +334,7 @@
     D = Dims(mesh, ly, lx, nc, width, nv)
     sites = D.sites
     field = (sites, nc, width)
-    vecs = vectors.reshape(nv, sites, 2 * nc).transpose(1, 0, 2)
+    vecs = vectors.reshape(nv, sites, 2 * nc).transpose(1, 2, 0)
     any_spec = pl.BlockSpec(memory_space=pl.ANY)
     vmem = pl.BlockSpec(memory_space=pltpu.VMEM)
     dma = pltpu.SemaphoreType.DMA
@@ -348,7 +348,7 @@
             pltpu.VMEM((nine, sites, nc, 2 * nc), F32),
             pltpu.VMEM(field, F32),
             pltpu.VMEM(field, F32),
-            pltpu.VMEM((sites, nv, 2 * nc), F32),
+            pltpu.VMEM((sites, 2 * nc, nv), F32),
             pltpu.VMEM(field, F32),
             dma((4,)),
             pltpu.VMEM((sites, 10 * nc, 2 * nc), BF16),
@@ -366,6 +366,7 @@
             pltpu.VMEM((ITERS, D.half, width), F32),
             pltpu.VMEM((ITERS, D.members, D.rows, width), F32),
             pltpu.VMEM((ITERS, nv, width), F32),
+            pltpu.VMEM((nv, 8), F32),
             dma((ITERS, 4, sites)),
             dma((ITERS, 4, sites)),
             dma((ITERS,)),
@@ -378,14 +379,14 @@
             dma((ITERS, D.pieces)),
         ],
         compiler_params=pltpu.CompilerParams(
-            collective_id=0, has_side_effects=True, vmem_limit_bytes=60 * 1024 * 1024
+            collective_id=0, has_side_effects=True, vmem_limit_bytes=50000 * 1024
         ),
     )(
         couplings.reshape(nine, sites, nc, 2 * nc),
         source.reshape(field),
         initial.reshape(field),
         vecs,
-        inverse_eigen.T,
+        inverse_eigen,
     )
     return x.reshape(source.shape), r.reshape(source.shape)
 

time: 131 us -> 123 us (0.939)
  local copies, waits for them, and re-layouts: 10.6 us -> 4.71 us
  Pallas kernels: 119 us -> 117 us
    unnamed x4 -> x8, local copies, waits for them, and re-layouts: 10.6 us -> 4.71 us
    pallas_call x1, Pallas kernels: 119 us -> 117 us  [solve(): pl.pallas_call(functools.partial(kernel, D), out_shape=(out, out), in_spe...]
where the time goes in v3:
time: 123 us
  Pallas kernels  117 us (95%)
  local copies, waits for them, and re-layouts  4.71 us (4%)
    pallas_call x1, Pallas kernels, solve(): pl.pallas_call(functools.partial(kernel, D), out_shape=(out, out), in_spe...  117 us
    unnamed x8, local copies, waits for them, and re-layouts  4.71 us

profile of v3, /device:TPU:1, one launch (start us, length us, event | category | flops | bytes accessed | tf_op | source)
XLA Modules:
  0.0 122.5 jit_solution(17061045128844363121)
XLA Ops:
  0.6 0.0 copy-start
  0.6 1.1 copy-done
  1.8 0.0 copy-start.1
  1.8 1.1 copy-done.1
  2.9 0.0 copy-start.2
  2.9 0.7 copy-done.2
  3.6 117.2 %shard_map.68 = (f32[8,96,256]{2,1,0:T(8,128)S(1)}, f32[8,96,256]{2,1,0:T(8,128)S(1)}) custom-call(f32[9,8,96,192]{3,2,1,0:T(8,128)} %bitcast.12, f32[8,96,256]{2,1,0:T(8,128)S(1)} %bitcast.10, f32[8,96,256]{2,1,0:T(8,128)S(1)} %bitcast.11, f32[8,192,512]{2,1,0:T(8,128)} %bitcast.13, f32[2,512]{1,0:T(2,128)S(1)} %copy-done.2), custom_call_target="tpu_custom_call" | custom-call | tf_op jit(solution)/shard_map/pallas_call | solution.py:342
  120.8 0.9 copy.9
  121.6 0.9 copy.10
Async XLA Ops:
  0.6 1.1 copy-start
  1.8 1.1 copy-start.1
  2.9 0.7 copy-start.2
